TPU v7x, 256 devices: a whole 4x4x8 slice. The times are simulated.
256 devices in a mesh: wide: 64 (over y, z, core), narrow: 4 (over x).
Axes of the slice: x: 4, y: 4, z: 8, core: 2. Of those that a mesh axis runs over, the one named last changes fastest.
Arguments:
- diag_block: float32 [256, 512, 512], P('wide', None, 'narrow'), as said below
- panel: float32 [256, 1024, 512], P('wide', None, 'narrow'), may hold values from -2 to 2
- panel_count: int32 [256], P('wide'), may hold values from 1 to 8, 1152 in all
- pair_owner: int32 [9216, 1], P('wide'), may hold values from 0 to 63; in each aligned block of 144 rows (0 to 143, 144 to 287, ...) at most 3 rows name the same one
- pair_slot: int32 [9216], P('wide'), may hold values from 0 to 7
- ancestor: float32 [512, 128, 128], P(('wide', 'narrow')), may hold values from -6 to 6
Outputs:
- factor: float32 [256, 512, 512], P('wide', None, 'narrow')
- lower_panel: float32 [256, 1024, 512], P('wide', None, 'narrow')
- updated: float32 [512, 128, 128], P(('wide', 'narrow'))
Inputs may be any that keep to these rules, and one draw needn't show every extreme that they name: Each diag_block[s] is symmetric, and its least eigenvalue is 0.2 or more. `pair_owner`: among the rows of one index of wide no owner is named more than 3 times, a bound that some block reaches.
All inputs are finite; a program needn't handle non-finite values. No bound on the sum of `panel_count` on one device may be relied on, other than what follows from the above.
Results may differ from a plain program's by a relative error of at most 0.00016.
Values sent between devices are 32-bit elements; how exact they have to be, the bound alone decides.
A program may use at most 128 MiB of HBM per device.

v0:
```python
import jax
import jax.numpy as jnp
import numpy as np
from jax import lax
from jax.sharding import PartitionSpec as P

W = 512
B = 128
P_SIZE = 8
T_DEV = 2


def pair_lists(count):
    first = []
    second = []
    for outer in range(count):
        for inner in range(outer + 1):
            first.append(outer)
            second.append(inner)
    return (np.array(first, np.int32), np.array(second, np.int32))


def local(diag_block, panel, panel_count, pair_owner, pair_slot, ancestor):
    supers_here = diag_block.shape[0]
    col_width = diag_block.shape[2]
    narrow_index = lax.axis_index("narrow")
    narrow_count = lax.axis_size("narrow")
    wide_count = lax.axis_size("wide")
    col_start = narrow_index * col_width
    whole_diag = lax.all_gather(diag_block, "narrow", axis=2, tiled=True)
    factor = jnp.linalg.cholesky(whole_diag)
    identity = jnp.broadcast_to(jnp.eye(W, dtype=jnp.float32), factor.shape)
    inverse = lax.linalg.triangular_solve(factor, identity, left_side=True, lower=True)
    inverse_t = jnp.swapaxes(inverse, 1, 2)
    own_cols = lax.dynamic_slice_in_dim(inverse_t, col_start, col_width, 2)
    lower_panel = jnp.einsum(
        "srk,skc->src",
        lax.all_gather(panel, "narrow", axis=2, tiled=True),
        own_cols,
        precision=lax.Precision.HIGHEST,
    )
    block_index = jnp.arange(P_SIZE * B, dtype=jnp.int32) // B
    live = (block_index[None, :] < panel_count[:, None]).astype(jnp.float32)
    lower_panel = lower_panel * live[:, :, None]
    first, second = pair_lists(P_SIZE)
    blocks = lower_panel.reshape(supers_here, P_SIZE, B, col_width)
    partial_updates = jnp.einsum(
        "spac,spbc->spab", blocks[:, first], blocks[:, second], precision=lax.Precision.HIGHEST
    )
    pair_rows = supers_here * len(first)
    partial_updates = partial_updates.reshape(pair_rows, B, B)
    capacity = max(2, (pair_rows + wide_count - 1) // wide_count)
    owners = pair_owner[:, 0]
    owner_table = (owners[:, None] == jnp.arange(wide_count, dtype=jnp.int32)[None, :]).astype(
        jnp.int32
    )
    earlier = jnp.cumsum(owner_table, axis=0) - owner_table
    rank_here = jnp.sum(earlier * owner_table, axis=1)
    position = owners * capacity + rank_here
    buffer_rows = wide_count * capacity
    row_slots = T_DEV * narrow_count
    slot_ids = jnp.full((buffer_rows,), -1, jnp.int32).at[position].set(pair_slot)
    send_buffer = jnp.zeros((buffer_rows, B, B), jnp.float32).at[position].set(partial_updates)
    received, got_slots = (
        lax.all_to_all(send_buffer, "wide", split_axis=0, concat_axis=0, tiled=True),
        lax.all_to_all(slot_ids, "wide", split_axis=0, concat_axis=0, tiled=True),
    )
    slot_table = (got_slots[:, None] == jnp.arange(row_slots, dtype=jnp.int32)[None, :]).astype(
        jnp.float32
    )
    row_sums = jnp.einsum("ri,rab->iab", slot_table, received, precision=lax.Precision.HIGHEST)
    summed = lax.psum_scatter(row_sums, "narrow", scatter_dimension=0, tiled=True)
    factor_cols = lax.dynamic_slice_in_dim(factor, col_start, col_width, 2)
    return (factor_cols, lower_panel, ancestor - summed)


def solution(mesh):
    placed = (
        P("wide", None, "narrow"),
        P("wide", None, "narrow"),
        P("wide"),
        P("wide", None),
        P("wide"),
        P(("wide", "narrow"), None, None),
    )
    return jax.shard_map(
        local,
        mesh=mesh,
        in_specs=placed,
        out_specs=(
            P("wide", None, "narrow"),
            P("wide", None, "narrow"),
            P(("wide", "narrow"), None, None),
        ),
        check_vma=False,
    )
```

profile of v0, /device:TPU:8, one launch (start us, length us, event | category | flops | bytes accessed | tf_op | source)
XLA Modules:
  0.0 1013.3 jit_solution(1670821156970173186)
XLA Ops:
  7.3 2.5 copy.74
  9.9 0.7 all-gather.5.cloned.1.call-update
  10.6 0.6 reduce-window.6
  11.2 0.2 slice_reduce_fusion
  11.6 1.2 scatter_custom_fusion
  12.8 0.8 all_to_all.9
  13.6 12.4 %all-to-all-start = ((s32[64,3,1]{1,2,0:T(1,128)}), s32[64,3,1]{1,2,0:T(1,128)S(1)}, u32[]{:S(2)}, u32[]{:S(2)}) async-start(s32[64,3,1]{1,2,0:T(1,128)} %bitcast.20), calls=%async_computation | async-start | bytes 65536 | tf_op jit(solution)/shard_map/all_to_all | solution.py:66
  26.4 0.8 fusion.61
  27.2 36.9 %all-gather.3.cloned.1.call-done = f32[4,512,512]{1,2,0:T(8,128)} async-done(((f32[4,512,128]{1,2,0:T(8,128)}), f32[4,512,512]{1,2,0:T(8,128)}) %all-gather.3.cloned.1.call-update) | async-done | bytes 4194320 | tf_op jit(solution)/shard_map/all_gather | solution.py:30
  64.1 5.3 copy.75
  69.4 4.5 fusion.5
  73.9 2.0 copy-done.1
  75.9 46.9 %custom-call.34 = f32[4,128,128]{2,1,0:T(8,128)S(1)} custom-call(f32[4,128,128]{2,1,0:T(8,128)S(1)} %cholesky.274), custom_call_target="Cholesky" | custom-call | tf_op jit(solution)/shard_map/jit(cholesky)/cholesky | solution.py:31
  122.8 39.3 %custom-call.35 = f32[4,1,128,128]{2,3,1,0:T(8,128)S(1)} custom-call(f32[4,1,128,128]{3,2,1,0:T(8,128)S(1)} %select_bitcast_fusion.2), custom_call_target="InvertDiagBlocksLowerTriangular" | custom-call | tf_op jit(solution)/shard_map/jit(cholesky)/cholesky | solution.py:31
  162.2 2.5 cholesky.234
  164.7 3.0 constant_dynamic-update-slice_fusion.3
  167.6 2.0 convolution_subtract_fusion.1
  169.6 47.1 %custom-call.36 = f32[4,128,128]{2,1,0:T(8,128)S(1)} custom-call(f32[4,128,128]{2,1,0:T(8,128)S(1)} %cholesky.278), custom_call_target="Cholesky" | custom-call | tf_op jit(solution)/shard_map/jit(cholesky)/cholesky | solution.py:31
  216.8 0.8 select_bitcast_fusion.1
  217.6 39.3 %custom-call.37 = f32[4,1,128,128]{2,3,1,0:T(8,128)S(1)} custom-call(f32[4,1,128,128]{3,2,1,0:T(8,128)S(1)} %get-tuple-element.46), custom_call_target="InvertDiagBlocksLowerTriangular" | custom-call | tf_op jit(solution)/shard_map/jit(cholesky)/cholesky | solution.py:31
  256.9 1.4 convolution_dynamic-update-slice_fusion
  258.3 2.6 convolution_subtract_fusion.2
  260.9 46.9 %custom-call.38 = f32[4,128,128]{2,1,0:T(8,128)S(1)} custom-call(f32[4,128,128]{2,1,0:T(8,128)S(1)} %cholesky.283), custom_call_target="Cholesky" | custom-call | tf_op jit(solution)/shard_map/jit(cholesky)/cholesky | solution.py:31
  307.8 0.8 select_bitcast_fusion
  308.6 39.8 %custom-call.39 = f32[4,1,128,128]{2,3,1,0:T(8,128)S(1)} custom-call(f32[4,1,128,128]{3,2,1,0:T(8,128)S(1)} %get-tuple-element.44), custom_call_target="InvertDiagBlocksLowerTriangular" | custom-call | tf_op jit(solution)/shard_map/jit(cholesky)/cholesky | solution.py:31
  348.4 1.1 convolution_dynamic-update-slice_fusion.1
  349.5 2.6 convolution_subtract_fusion.3
  352.1 46.9 %custom-call.40 = f32[4,128,128]{2,1,0:T(8,128)S(1)} custom-call(f32[4,128,128]{2,1,0:T(8,128)S(1)} %convolution_subtract_fusion.3), custom_call_target="Cholesky" | custom-call | tf_op jit(solution)/shard_map/jit(cholesky)/cholesky | solution.py:31
  399.0 0.8 select_reduce_fusion.2
  400.0 0.2 compare_reduce_fusion
  400.2 6.7 broadcast_select_fusion
  406.9 15.0 %while.1 = (s32[]{:T(128)}, f32[4,512,512]{2,1,0:T(8,128)}, s32[4,2]{0,1:T(2,128)S(1)}, f32[4,4,128,128]{3,2,0,1:T(8,128)}, s32[]{:T(128)}) while((s32[]{:T(128)}, f32[4,512,512]{2,1,0:T(8,128)}, s32[4,2]{0,1:T(2,128)S(1)}, f32[4,4,128,128]{3,2,0,1:T(8,128)}, s32[]{:T(128)}) %tuple.40), condition=%wide.while_cond, body=%wide.while_body.sunk | while | flops 2 | bytes 525421 | solution.py:33
  407.0 0.5 fusion.71
  407.5 3.2 bitcast_dynamic-update-slice_fusion.2
  410.8 0.5 fusion.71
  411.3 3.2 bitcast_dynamic-update-slice_fusion.2
  414.6 0.5 fusion.71
  415.1 3.2 bitcast_dynamic-update-slice_fusion.2
  418.3 0.5 fusion.71
  418.9 3.1 bitcast_dynamic-update-slice_fusion.2
  421.9 158.2 %custom-call.41 = f32[4,4,128,128]{2,3,1,0:T(8,128)S(1)} custom-call(f32[4,4,128,128]{3,2,1,0:T(8,128)} %bitcast.100), custom_call_target="InvertDiagBlocksLowerTriangular" | custom-call | tf_op jit(solution)/shard_map/triangular_solve | solution.py:33
  580.1 1.0 fusion.35
  581.2 2.0 convolution_subtract_fusion
  583.1 1.1 fusion.40
  584.2 2.4 fusion.19
  586.7 2.0 fusion.38
  588.7 3.3 fusion.16
  592.0 3.1 fusion.37
  595.1 13.3 %multiply_bitcast_fusion = f32[4,1024,128]{1,2,0:T(8,128)} fusion(f32[4,1024,512]{2,1,0:T(8,128)} %all-gather.5.cloned.1.call-done, s32[]{:T(128)S(6)} %select_n.29, f32[4,128,512]{2,1,0:T(8,128)S(1)} %fusion.35, f32[4,128,512]{2,1,0:T(8,128)S(1)} %fusion.40, f32[4,128,512]{2,1,0:T(8,128)S(1)} %fusion.38, f32[4,128,512]{2,1,0:T(8,128)} %fusion.37, ...), kind=kOutput, calls=%fused_computation.28 | convolution fusion | flops 3222536192 | bytes 14696452 | tf_op jit(solution)/shard_map/srk,skc->src/dot_general | solution.py:36
  608.4 1.9 copy.96
  610.3 6.7 gather_fusion.1
  617.1 6.7 gather_fusion
  623.8 25.8 %fusion.2 = f32[4,36,128,128]{3,2,1,0:T(8,128)} fusion(f32[36,4,128,128]{3,2,1,0:T(8,128)} %gather_fusion.1, f32[36,4,128,128]{3,2,1,0:T(8,128)} %gather_fusion), kind=kOutput, calls=%fused_computation.8 | convolution fusion | flops 3623878656 | bytes 28311552 | tf_op jit(solution)/shard_map/spac,spbc->spab/dot_general | solution.py:47
  649.6 6.2 broadcast_in_dim.43
  655.7 26.3 %scatter_fusion = f32[192,128,128]{2,1,0:T(8,128)} fusion(f32[192,128,128]{2,1,0:T(8,128)} %broadcast_in_dim.43, s32[144]{0:T(256)S(1)} %bitcast.98, f32[144,128,128]{2,1,0:T(8,128)} %bitcast.94), kind=kCustom, calls=%fused_computation.3 | custom fusion | bytes 28312128 | tf_op jit(solution)/shard_map/scatter | solution.py:63
  682.1 10.7 %all-to-all-start.1 = ((f32[192,128,128]{2,1,0:T(8,128)}), f32[192,128,128]{2,1,0:T(8,128)}, u32[]{:S(2)}, u32[]{:S(2)}) async-start(f32[192,128,128]{2,1,0:T(8,128)} %scatter_fusion), calls=%async_computation.1 | async-start | bytes 25165824 | tf_op jit(solution)/shard_map/all_to_all | solution.py:65
  692.9 0.5 broadcast.291
  693.4 0.7 reduce.29
  694.2 273.1 %all-to-all-done.1 = f32[192,128,128]{2,1,0:T(8,128)} async-done(((f32[192,128,128]{2,1,0:T(8,128)}), f32[192,128,128]{2,1,0:T(8,128)}, u32[]{:S(2)}, u32[]{:S(2)}) %all-to-all-start.1) | async-done | bytes 12582944 | tf_op jit(solution)/shard_map/all_to_all | solution.py:65
  967.4 15.5 %fusion = f32[8,128,128]{2,0,1:T(8,128)S(1)} fusion(f32[192,128,128]{2,1,0:T(8,128)} %all-to-all-done.1, s32[192]{0:T(256)S(1)} %eq.54), kind=kOutput, calls=%fused_computation.6 | convolution fusion | flops 301991424 | bytes 13107968 | tf_op jit(solution)/shard_map/ri,rab->iab/dot_general | solution.py:71
  982.8 0.9 copy.95
  983.7 2.3 constant_dynamic-slice_fusion.1
  986.0 18.7 %reduce-scatter.2.cloned.1.call-done = f32[2,128,128]{2,1,0:T(8,128)} async-done(((f32[8,128,128]{2,1,0:T(8,128)}), f32[2,128,128]{2,1,0:T(8,128)}) %reduce-scatter.2.cloned.1.call-update) | async-done | bytes 131088 | tf_op jit(solution)/shard_map/reduce_scatter | solution.py:72
  1004.7 1.6 sub.14
  (51 shorter events, 1.4 us)
Async XLA Ops:
  7.2 18.9 %copy-start.6 = (s32[36]{0:T(128)S(1)}, s32[36]{0:T(128)}, u32[]{:S(2)}) copy-start(s32[36]{0:T(128)} %constant.237) | copy-start | bytes 436
  7.2 18.9 %copy-start.5 = (s32[36]{0:T(128)S(1)}, s32[36]{0:T(128)}, u32[]{:S(2)}) copy-start(s32[36]{0:T(128)} %constant.238) | copy-start | bytes 436
  7.2 3.4 copy-start.4
  7.2 19.1 %copy-start.7 = (s32[4]{0:T(128)S(1)}, s32[4]{0:T(128)}, u32[]{:S(2)}) copy-start(s32[4]{0:T(128)} %param.12) | copy-start | bytes 52
  7.2 56.9 %all-gather.3.cloned.1.call-start = ((), (), s32[]{:S(2)}) async-start(), calls=%async_computation.3 | async-start | bytes 5242880 | tf_op jit(solution)/shard_map/all_gather | solution.py:30
  9.8 585.3 %all-gather.5.cloned.1.call-start = ((), (), s32[]{:S(2)}) async-start(), calls=%async_computation.4 | async-start | bytes 10485760 | tf_op jit(solution)/shard_map/all_gather | solution.py:38
  13.6 668.5 %all-to-all-start = ((s32[64,3,1]{1,2,0:T(1,128)}), s32[64,3,1]{1,2,0:T(1,128)S(1)}, u32[]{:S(2)}, u32[]{:S(2)}) async-start(s32[64,3,1]{1,2,0:T(1,128)} %bitcast.20), calls=%async_computation | async-start | bytes 65536 | tf_op jit(solution)/shard_map/all_to_all | solution.py:66
  73.9 2.0 copy-start.1
  580.1 4.1 copy-start.2
  610.3 6.8 copy-start
  682.1 285.3 %all-to-all-start.1 = ((f32[192,128,128]{2,1,0:T(8,128)}), f32[192,128,128]{2,1,0:T(8,128)}, u32[]{:S(2)}, u32[]{:S(2)}) async-start(f32[192,128,128]{2,1,0:T(8,128)} %scatter_fusion), calls=%async_computation.1 | async-start | bytes 25165824 | tf_op jit(solution)/shard_map/all_to_all | solution.py:65
  692.8 311.9 %reduce-scatter.2.cloned.1.call-start = ((), (), s32[]{:S(2)}) async-start(), calls=%async_computation.5 | async-start | bytes 655360 | tf_op jit(solution)/shard_map/reduce_scatter | solution.py:72
  694.2 310.5 %copy-start.3 = (f32[2,128,128]{2,1,0:T(8,128)S(1)}, f32[2,128,128]{2,1,0:T(8,128)}, u32[]{:S(2)}) copy-start(f32[2,128,128]{2,1,0:T(8,128)} %param.15) | copy-start | bytes 393220
Sparse Core Ops, SparseCore 0:
  10.4 53.6 all-gather.2
  65.9 90.4 all-gather.4
  983.9 20.7 reduce-scatter.1
where the time goes:
time: 1020 us; the launch traced here: 1010 us
  other arithmetic  482 us (47%)
  waiting for transfers between devices  329 us (32%)
  matrix products  82.2 us (8%)
  local copies, waits for them, and re-layouts  82 us (8%)
  starting transfers between devices  23.3 us (2%)
  between operations  14.6 us (1%)
    another operation x16, other arithmetic, local(): factor = jnp.linalg.cholesky(whole_diag)  309 us
    all_to_all x1, waiting for transfers between devices, local(): lax.all_to_all(send_buffer, 'wide', split_axis=0, concat_axis=0, tiled=True)  273 us
    another operation x3, other arithmetic, local(): lax.linalg.triangular_solve(factor, identity, left_side=True, lower=True)  165 us
    all_gather x1, waiting for transfers between devices, local(): whole_diag = lax.all_gather(diag_block, 'narrow', axis=2, tiled=True)  36.9 us
    scatter x1, local copies, waits for them, and re-layouts, local(): jnp.zeros((buffer_rows, B, B), jnp.float32).at[position]  26.3 us
    dot_general x1, matrix products, local(): jnp.einsum('spac,spbc->spab', blocks[:, first], blocks[:, second], precis...  25.8 us
  transfers between devices with their start and end apart: 5, of which 3 were waited for; matrix products, arithmetic and copies ran while one was open for 61% of the time, Pallas kernels for 0%

commit v1 on v0

--- a/solution.py
+++ b/solution.py
@@ -27,7 +27,25 @@
     narrow_count = lax.axis_size("narrow")
     wide_count = lax.axis_size("wide")
     col_start = narrow_index * col_width
-    whole_diag = lax.all_gather(diag_block, "narrow", axis=2, tiled=True)
+    devices, index, span = (lax.axis_size("narrow"), lax.axis_index("narrow"), diag_block.shape[2])
+    ahead = [(i, (i + 1) % devices) for i in range(devices)]
+    left = [(i, (i - 1) % devices) for i in range(devices)]
+    whole_diag = jnp.zeros(
+        (*diag_block.shape[:2], devices * span, *diag_block.shape[2 + 1 :]), diag_block.dtype
+    )
+    whole_diag = lax.dynamic_update_slice_in_dim(whole_diag, diag_block, index * span, axis=2)
+    from_left = from_right = diag_block
+    half = devices // 2
+    for step in range(1, half + 1):
+        from_left = lax.ppermute(from_left, "narrow", ahead)
+        whole_diag = lax.dynamic_update_slice_in_dim(
+            whole_diag, from_left, (index - step) % devices * span, axis=2
+        )
+        if step < devices - half:
+            from_right = lax.ppermute(from_right, "narrow", left)
+            whole_diag = lax.dynamic_update_slice_in_dim(
+                whole_diag, from_right, (index + step) % devices * span, axis=2
+            )
     factor = jnp.linalg.cholesky(whole_diag)
     identity = jnp.broadcast_to(jnp.eye(W, dtype=jnp.float32), factor.shape)
     inverse = lax.linalg.triangular_solve(factor, identity, left_side=True, lower=True)

time: 1020 us -> 1050 us (1.029)
  waiting for transfers between devices: 329 us -> 349 us
  local copies, waits for them, and re-layouts: 82 us -> 92.7 us
    ppermute x0 -> x3, waiting for transfers between devices: none -> 58.3 us  [the longest x2 58.3 us: local(): from_left = lax.ppermute(from_left, 'narrow', ahead)]
    all_gather x1 -> x0, waiting for transfers between devices: 36.9 us -> none  [local(): whole_diag = lax.all_gather(diag_block, 'narrow', axis=2, tiled=True)]
    dynamic_update_slice x0 -> x5, local copies, waits for them, and re-layouts: none -> 10.7 us  [the longest x3 8.61 us: local(): lax.dynamic_update_slice_in_dim(whole_diag, from_left, (index - step) % d...]
  transfers between devices with their start and end apart: 5 -> 7, of which waited for: 3 -> 4; matrix products, arithmetic and copies ran while one was open for 61% -> 60% of each run, Pallas kernels for 0% -> 0%
where the time goes in v1:
time: 1050 us
  other arithmetic  480 us (46%)
  waiting for transfers between devices  349 us (33%)
  local copies, waits for them, and re-layouts  92.7 us (9%)
  matrix products  81.4 us (8%)
  starting transfers between devices  29 us (3%)
  between operations  15.1 us (1%)
    another operation x16, other arithmetic, local(): factor = jnp.linalg.cholesky(whole_diag)  307 us
    all_to_all x1, waiting for transfers between devices, local(): lax.all_to_all(send_buffer, 'wide', split_axis=0, concat_axis=0, tiled=True)  273 us
    another operation x3, other arithmetic, local(): lax.linalg.triangular_solve(factor, identity, left_side=True, lower=True)  165 us
    ppermute x2, waiting for transfers between devices, local(): from_left = lax.ppermute(from_left, 'narrow', ahead)  58.3 us
    scatter x1, local copies, waits for them, and re-layouts, local(): jnp.zeros((buffer_rows, B, B), jnp.float32).at[position]  26.3 us
    dot_general x1, matrix products, local(): jnp.einsum('spac,spbc->spab', blocks[:, first], blocks[:, second], precis...  25.8 us
  transfers between devices with their start and end apart: 7, of which 4 were waited for; matrix products, arithmetic and copies ran while one was open for 60% of the time, Pallas kernels for 0%

profile of v1, /device:TPU:8, one launch (start us, length us, event | category | flops | bytes accessed | tf_op | source)
XLA Modules:
  0.0 1046.8 jit_solution(130999223497582267)
XLA Ops:
  7.9 1.6 copy.122
  9.5 2.8 collective-permute-start.1
  13.4 1.2 scatter_custom_fusion
  14.6 0.8 all_to_all.9
  15.3 12.1 %all-to-all-start = ((s32[64,3,1]{1,2,0:T(1,128)}), s32[64,3,1]{1,2,0:T(1,128)S(1)}, u32[]{:S(2)}, u32[]{:S(2)}) async-start(s32[64,3,1]{1,2,0:T(1,128)} %bitcast.20), calls=%async_computation | async-start | bytes 65536 | tf_op jit(solution)/shard_map/all_to_all | solution.py:84
  27.6 19.5 %collective-permute-done = f32[4,512,128]{1,2,0:T(8,128)S(1)} collective-permute-done((f32[4,512,128]{1,2,0:T(8,128)S(1)}, f32[4,512,128]{1,2,0:T(8,128)S(1)}, u32[]{:S(2)}, u32[]{:S(2)}) %collective-permute-start) | collective-permute-done | bytes 1048608 | tf_op jit(solution)/shard_map/ppermute | solution.py:40
  47.6 2.5 broadcast_in_dim.41
  50.1 1.0 constant_dynamic-update-slice_fusion.7
  51.2 1.0 fusion.66
  52.2 1.1 constant_dynamic-update-slice_fusion.6
  53.2 1.0 constant_dynamic-update-slice_fusion.5
  54.3 38.8 %collective-permute-done.2 = f32[4,512,128]{1,2,0:T(8,128)} collective-permute-done((f32[4,512,128]{1,2,0:T(8,128)S(1)}, f32[4,512,128]{1,2,0:T(8,128)}, u32[]{:S(2)}, u32[]{:S(2)}) %collective-permute-start.2) | collective-permute-done | bytes 1048608 | tf_op jit(solution)/shard_map/ppermute | solution.py:40
  93.0 2.3 constant_dynamic-update-slice_fusion.4
  95.3 5.3 copy.125
  100.6 4.5 fusion.5
  105.1 2.0 copy-done.2
  107.1 46.9 %custom-call.34 = f32[4,128,128]{2,1,0:T(8,128)S(1)} custom-call(f32[4,128,128]{2,1,0:T(8,128)S(1)} %cholesky.271), custom_call_target="Cholesky" | custom-call | tf_op jit(solution)/shard_map/jit(cholesky)/cholesky | solution.py:49
  154.2 39.3 %custom-call.35 = f32[4,1,128,128]{2,3,1,0:T(8,128)S(1)} custom-call(f32[4,1,128,128]{3,2,1,0:T(8,128)S(1)} %select_bitcast_fusion.2), custom_call_target="InvertDiagBlocksLowerTriangular" | custom-call | tf_op jit(solution)/shard_map/jit(cholesky)/cholesky | solution.py:49
  193.5 2.0 fusion.32
  195.8 2.0 slice_subtract_fusion
  197.8 47.1 %custom-call.36 = f32[4,128,128]{2,1,0:T(8,128)S(1)} custom-call(f32[4,128,128]{2,1,0:T(8,128)S(1)} %cholesky.275), custom_call_target="Cholesky" | custom-call | tf_op jit(solution)/shard_map/jit(cholesky)/cholesky | solution.py:49
  245.1 39.3 %custom-call.37 = f32[4,1,128,128]{2,3,1,0:T(8,128)S(1)} custom-call(f32[4,1,128,128]{3,2,1,0:T(8,128)S(1)} %select_bitcast_fusion.1), custom_call_target="InvertDiagBlocksLowerTriangular" | custom-call | tf_op jit(solution)/shard_map/jit(cholesky)/cholesky | solution.py:49
  285.7 1.9 copy-done.1
  287.7 2.9 slice_subtract_fusion.1
  290.6 47.4 %custom-call.38 = f32[4,128,128]{2,1,0:T(8,128)S(1)} custom-call(f32[4,128,128]{2,1,0:T(8,128)S(1)} %cholesky.280), custom_call_target="Cholesky" | custom-call | tf_op jit(solution)/shard_map/jit(cholesky)/cholesky | solution.py:49
  338.2 39.3 %custom-call.39 = f32[4,1,128,128]{2,3,1,0:T(8,128)S(1)} custom-call(f32[4,1,128,128]{3,2,1,0:T(8,128)S(1)} %select_bitcast_fusion), custom_call_target="InvertDiagBlocksLowerTriangular" | custom-call | tf_op jit(solution)/shard_map/jit(cholesky)/cholesky | solution.py:49
  377.5 0.7 constant_dynamic-update-slice_fusion.1
  378.2 1.3 convolution_dynamic-update-slice_fusion.1
  379.5 2.9 slice_subtract_fusion.2
  382.4 46.9 %custom-call.40 = f32[4,128,128]{2,1,0:T(8,128)S(1)} custom-call(f32[4,128,128]{2,1,0:T(8,128)S(1)} %slice_subtract_fusion.2), custom_call_target="Cholesky" | custom-call | tf_op jit(solution)/shard_map/jit(cholesky)/cholesky | solution.py:49
  429.9 0.7 constant_dynamic-update-slice_fusion
  430.6 6.7 broadcast_select_fusion
  437.4 15.9 %while.1 = (s32[]{:T(128)}, f32[4,512,512]{1,2,0:T(8,128)}, s32[4,2]{0,1:T(2,128)S(1)}, f32[4,4,128,128]{3,2,0,1:T(8,128)}, s32[]{:T(128)}) while((s32[]{:T(128)}, f32[4,512,512]{1,2,0:T(8,128)}, s32[4,2]{0,1:T(2,128)S(1)}, f32[4,4,128,128]{3,2,0,1:T(8,128)}, s32[]{:T(128)}) %tuple.40), condition=%wide.while_cond, body=%wide.while_body.sunk | while | flops 2 | bytes 1572981 | solution.py:51
  438.1 2.5 constant_dynamic-slice_fusion.6
  440.7 0.7 bitcast_dynamic-update-slice_fusion.2
  442.1 2.5 constant_dynamic-slice_fusion.6
  444.7 0.7 bitcast_dynamic-update-slice_fusion.2
  446.1 2.5 constant_dynamic-slice_fusion.6
  448.7 0.7 bitcast_dynamic-update-slice_fusion.2
  450.1 2.4 constant_dynamic-slice_fusion.6
  452.6 0.7 bitcast_dynamic-update-slice_fusion.2
  453.3 158.2 %custom-call.41 = f32[4,4,128,128]{2,3,1,0:T(8,128)S(1)} custom-call(f32[4,4,128,128]{3,2,1,0:T(8,128)} %bitcast.98), custom_call_target="InvertDiagBlocksLowerTriangular" | custom-call | tf_op jit(solution)/shard_map/triangular_solve | solution.py:51
  611.6 1.0 fusion.37
  612.6 2.0 convolution_subtract_fusion
  614.7 1.1 fusion.42
  615.8 2.5 fusion.19
  618.3 2.0 fusion.40
  620.3 3.3 fusion.16
  623.6 3.1 fusion.39
  626.8 13.3 %multiply_bitcast_fusion = f32[4,1024,128]{1,2,0:T(8,128)} fusion(f32[4,1024,512]{2,1,0:T(8,128)} %all-gather.2.cloned.1.call-done, s32[]{:T(128)S(6)} %select_n.53, f32[4,128,512]{2,1,0:T(8,128)S(1)} %fusion.37, f32[4,128,512]{2,1,0:T(8,128)S(1)} %fusion.42, f32[4,128,512]{2,1,0:T(8,128)S(1)} %fusion.40, f32[4,128,512]{2,1,0:T(8,128)} %fusion.39, ...), kind=kOutput, calls=%fused_computation.29 | convolution fusion | flops 3222536192 | bytes 14696452 | tf_op jit(solution)/shard_map/srk,skc->src/dot_general | solution.py:54
  640.0 1.9 copy.162
  642.0 6.7 gather_fusion.1
  648.7 6.7 gather_fusion
  655.4 25.8 %fusion.2 = f32[4,36,128,128]{3,2,1,0:T(8,128)} fusion(f32[36,4,128,128]{3,2,1,0:T(8,128)} %gather_fusion.1, f32[36,4,128,128]{3,2,1,0:T(8,128)} %gather_fusion), kind=kOutput, calls=%fused_computation.9 | convolution fusion | flops 3623878656 | bytes 28311552 | tf_op jit(solution)/shard_map/spac,spbc->spab/dot_general | solution.py:65
  681.2 6.2 broadcast_in_dim.47
  687.4 26.3 %scatter_fusion = f32[192,128,128]{2,1,0:T(8,128)} fusion(f32[192,128,128]{2,1,0:T(8,128)} %broadcast_in_dim.47, s32[144]{0:T(256)S(1)} %bitcast.96, f32[144,128,128]{2,1,0:T(8,128)} %bitcast.92), kind=kCustom, calls=%fused_computation.3 | custom fusion | bytes 28312128 | tf_op jit(solution)/shard_map/scatter | solution.py:81
  713.7 13.8 %all-to-all-start.1 = ((f32[192,128,128]{2,1,0:T(8,128)}), f32[192,128,128]{2,1,0:T(8,128)}, u32[]{:S(2)}, u32[]{:S(2)}) async-start(f32[192,128,128]{2,1,0:T(8,128)} %scatter_fusion), calls=%async_computation.1 | async-start | bytes 25165824 | tf_op jit(solution)/shard_map/all_to_all | solution.py:83
  728.9 273.1 %all-to-all-done.1 = f32[192,128,128]{2,1,0:T(8,128)} async-done(((f32[192,128,128]{2,1,0:T(8,128)}), f32[192,128,128]{2,1,0:T(8,128)}, u32[]{:S(2)}, u32[]{:S(2)}) %all-to-all-start.1) | async-done | bytes 12582944 | tf_op jit(solution)/shard_map/all_to_all | solution.py:83
  1002.0 15.5 %fusion = f32[8,128,128]{2,0,1:T(8,128)S(1)} fusion(f32[192,128,128]{2,1,0:T(8,128)} %all-to-all-done.1, s32[192]{0:T(256)S(1)} %eq.58), kind=kOutput, calls=%fused_computation.7 | convolution fusion | flops 301991424 | bytes 13107968 | tf_op jit(solution)/shard_map/ri,rab->iab/dot_general | solution.py:89
  1017.5 0.9 copy.160
  1018.4 1.3 constant_dynamic-slice_fusion.2
  1019.7 1.3 copy.161
  1021.1 16.9 %reduce-scatter.2.cloned.1.call-done = f32[2,128,128]{2,1,0:T(8,128)} async-done(((f32[8,128,128]{2,1,0:T(8,128)}), f32[2,128,128]{2,1,0:T(8,128)}) %reduce-scatter.2.cloned.1.call-update) | async-done | bytes 131088 | tf_op jit(solution)/shard_map/reduce_scatter | solution.py:90
  1037.9 1.6 sub.22
  (87 shorter events, 9.5 us)
Async XLA Ops:
  7.2 20.3 %copy-start.11 = (s32[36]{0:T(128)S(1)}, s32[36]{0:T(128)}, u32[]{:S(2)}) copy-start(s32[36]{0:T(128)} %constant.262) | copy-start | bytes 436
  7.2 20.4 %copy-start.10 = (s32[36]{0:T(128)S(1)}, s32[36]{0:T(128)}, u32[]{:S(2)}) copy-start(s32[36]{0:T(128)} %constant.263) | copy-start | bytes 436
  7.2 5.2 copy-start.9
  7.2 619.6 %all-gather.2.cloned.1.call-start = ((), (), s32[]{:S(2)}) async-start(), calls=%async_computation.3 | async-start | bytes 10485760 | tf_op jit(solution)/shard_map/all_gather | solution.py:56
  9.5 41.6 %copy-start.12 = (s32[4]{0:T(128)S(1)}, s32[4]{0:T(128)}, u32[]{:S(2)}) copy-start(s32[4]{0:T(128)} %param.12) | copy-start | bytes 52
  9.5 43.7 %collective-permute-start.1 = (f32[4,512,128]{1,2,0:T(8,128)S(1)}, f32[4,512,128]{1,2,0:T(8,128)S(1)}, u32[]{:S(2)}, u32[]{:S(2)}) collective-permute-start(f32[4,512,128]{1,2,0:T(8,128)S(1)} %copy.122), channel_id=1, source_target_pairs={{0,3},{1,0},{2,1},{3,2},{4,7},{5,4},{6,5},{7,6},{8,11},{9,8},{10,9... | collective-permute-start | bytes 3145736 | tf_op jit(solution)/shard_map/ppermute | solution.py:45
  12.3 34.8 %collective-permute-start = (f32[4,512,128]{1,2,0:T(8,128)S(1)}, f32[4,512,128]{1,2,0:T(8,128)S(1)}, u32[]{:S(2)}, u32[]{:S(2)}) collective-permute-start(f32[4,512,128]{1,2,0:T(8,128)S(1)} %copy.122), channel_id=1, source_target_pairs={{0,1},{1,2},{2,3},{3,0},{4,5},{5,6},{6,7},{7,4},{8,9},{9,10},{10,1... | collective-permute-start | bytes 3145736 | tf_op jit(solution)/shard_map/ppermute | solution.py:40
  15.3 698.3 %all-to-all-start = ((s32[64,3,1]{1,2,0:T(1,128)}), s32[64,3,1]{1,2,0:T(1,128)S(1)}, u32[]{:S(2)}, u32[]{:S(2)}) async-start(s32[64,3,1]{1,2,0:T(1,128)} %bitcast.20), calls=%async_computation | async-start | bytes 65536 | tf_op jit(solution)/shard_map/all_to_all | solution.py:84
  47.2 45.9 %collective-permute-start.2 = (f32[4,512,128]{1,2,0:T(8,128)S(1)}, f32[4,512,128]{1,2,0:T(8,128)}, u32[]{:S(2)}, u32[]{:S(2)}) collective-permute-start(f32[4,512,128]{1,2,0:T(8,128)S(1)} %collective-permute-done), channel_id=1, source_target_pairs={{0,1},{1,2},{2,3},{3,0},{4,5},{5,6},{6,7},{7,4},{8,9},{9,10},{10,1... | collective-permute-start | bytes 3145736 | tf_op jit(solution)/shard_map/ppermute | solution.py:40
  105.1 2.0 copy-start.2
  285.7 2.0 copy-start.1
  437.4 174.2 %copy-start.6 = (f32[128,512]{1,0:T(8,128)S(1)}, f32[128,512]{1,0:T(8,128)}, u32[]{:S(2)}) copy-start(f32[128,512]{1,0:T(8,128)} %get-tuple-element.58) | copy-start | bytes 786436
  437.4 175.2 %copy-start.5 = (f32[128,512]{1,0:T(8,128)S(1)}, f32[128,512]{1,0:T(8,128)}, u32[]{:S(2)}) copy-start(f32[128,512]{1,0:T(8,128)} %get-tuple-element.57) | copy-start | bytes 786436
  453.3 162.5 %copy-start.7 = (f32[128,512]{1,0:T(8,128)S(1)}, f32[128,512]{1,0:T(8,128)}, u32[]{:S(2)}) copy-start(f32[128,512]{1,0:T(8,128)} %get-tuple-element.56) | copy-start | bytes 786436
  611.5 4.2 copy-start.3
  614.7 5.6 copy-start.4
  641.9 6.8 copy-start
  713.7 288.4 %all-to-all-start.1 = ((f32[192,128,128]{2,1,0:T(8,128)}), f32[192,128,128]{2,1,0:T(8,128)}, u32[]{:S(2)}, u32[]{:S(2)}) async-start(f32[192,128,128]{2,1,0:T(8,128)} %scatter_fusion), calls=%async_computation.1 | async-start | bytes 25165824 | tf_op jit(solution)/shard_map/all_to_all | solution.py:83
  727.5 310.4 %reduce-scatter.2.cloned.1.call-start = ((), (), s32[]{:S(2)}) async-start(), calls=%async_computation.4 | async-start | bytes 655360 | tf_op jit(solution)/shard_map/reduce_scatter | solution.py:90
  1017.5 20.4 %copy-start.8 = (f32[2,128,128]{2,1,0:T(8,128)S(1)}, f32[2,128,128]{2,1,0:T(8,128)}, u32[]{:S(2)}) copy-start(f32[2,128,128]{2,1,0:T(8,128)} %param.15) | copy-start | bytes 393220
Sparse Core Ops, SparseCore 0:
  9.8 119.3 all-gather.1
  1018.6 19.3 reduce-scatter.1
